TPU v7x, 256 devices: a whole 4x4x8 slice. The times are simulated.
256 devices in a mesh: stream: 4 (over x), seq: 64 (over z, y, core).
Axes of the slice: x: 4, y: 4, z: 8, core: 2. Of those that a mesh axis runs over, the one named last changes fastest.
Arguments:
- inputs: bfloat16 [4, 8192, 2048], P('stream', 'seq'), may hold values from -16 to 16
- cotangent: bfloat16 [4, 8192, 2048], P('stream', 'seq'), may hold values from -6 to 6
- lengths: int32 [4, 4], P('stream'), may hold values from 1 to 6144, 8192 in all within a row
- angles: float32 [2, 2048], replicated, may hold values from -3.140625 to 3.140625
- mix: float32 [14, 2048], replicated, may hold values from -1.5 to 1.5
- weight: bfloat16 [2048, 2048], replicated, may hold values from -0.125 to 0.125
Outputs:
- output: bfloat16 [4, 8192, 2048], P('stream', 'seq')
- input_grad: bfloat16 [4, 8192, 2048], P('stream', 'seq')
- weight_grad: float32 [2048, 2048], P('seq')
- angle_grad: float32 [2, 2048], replicated
- mix_grad: float32 [14, 2048], replicated
Inputs may be any that keep to these rules, and one draw needn't show every extreme that they name: Each row holds the lengths of the 4 documents of one stream in time order; they sum to 8192, and the longest is exactly 6144.
All inputs are finite; a program needn't handle non-finite values.
Results may differ from a plain program's by a relative error of at most 0.012.
Values may be sent and summed in bfloat16 or wider, within the bound.
No kernel may reach another device: no remote copies, remote signals or barrier semaphores. Data moves between devices by JAX's collectives and lax.ppermute only.
A program may use at most 128 MiB of HBM per device.

v0:
```python
import jax
import jax.numpy as jnp
from jax import lax
from jax.sharding import PartitionSpec as P


def from_behind(block, axis, distance):
    devices = range(lax.axis_size(axis))
    route = [(i - distance, i) for i in devices if i - distance in devices]
    return lax.ppermute(block, axis, route)


def segment_start(lengths_row, times):
    ends = jnp.cumsum(lengths_row, dtype=jnp.int32)
    hits = jnp.where(ends[None, :] <= times[:, None], lengths_row[None, :], 0)
    return jnp.sum(hits, axis=1, dtype=jnp.int32)


def tap_mask(times, start, dist):
    return (times - dist >= start).astype(jnp.float32)


def body(inputs, cotangent, lengths, angles, mix, weight):
    local_in = inputs[0]
    local_cot = cotangent[0]
    rows, width = local_in.shape
    seq_count = lax.axis_size("seq")
    stream_count = lax.axis_size("stream")
    far_count = seq_count.bit_length() - 1
    near_count = rows.bit_length() - 1
    levels = near_count + far_count
    total = rows * seq_count
    factor = float(stream_count * total) ** (-0.5)
    member = lax.axis_index("seq")
    cos_a = jnp.cos(angles[0])
    sin_a = jnp.sin(angles[0])
    cos_d = jnp.cos(angles[1])
    sin_d = jnp.sin(angles[1])
    times = member * rows + jnp.arange(rows, dtype=jnp.int32)
    start = segment_start(lengths[0], times)
    masks = [tap_mask(times, start, 2**level)[:, None] for level in range(levels)]
    current = local_in
    stored = [current]
    taps = []
    mixed = jnp.zeros((rows, width), jnp.float32)
    for level in range(near_count):
        dist = 2**level
        before = from_behind(current[rows - dist :], "seq", 1)
        shifted = (
            jnp.concatenate([before, current[: rows - dist]], axis=0).astype(jnp.float32)
            * masks[level]
        )
        plain = current.astype(jnp.float32)
        mixed = mixed + mix[level] * (cos_d * plain + sin_d * shifted)
        current = lax.optimization_barrier((cos_a * plain + sin_a * shifted).astype(jnp.bfloat16))
        taps.append(shifted.astype(jnp.bfloat16))
        stored.append(current)
    for level in range(near_count, levels):
        dist = 2**level
        arrived = from_behind(current, "seq", dist // rows)
        shifted = arrived.astype(jnp.float32) * masks[level]
        plain = current.astype(jnp.float32)
        mixed = mixed + mix[level] * (cos_d * plain + sin_d * shifted)
        current = lax.optimization_barrier((cos_a * plain + sin_a * shifted).astype(jnp.bfloat16))
        taps.append(shifted.astype(jnp.bfloat16))
        stored.append(current)
    mixed = mixed + mix[levels] * current.astype(jnp.float32)
    act = jax.nn.gelu(mixed).astype(jnp.bfloat16)
    output = jnp.dot(act, weight, preferred_element_type=jnp.float32).astype(jnp.bfloat16)
    act_grad = lax.optimization_barrier(
        lax.dot_general(
            local_cot, weight, (((1,), (1,)), ((), ())), preferred_element_type=jnp.float32
        ).astype(jnp.bfloat16)
    )
    unused, pull = jax.vjp(jax.nn.gelu, mixed)
    mixed_grad = lax.optimization_barrier(
        pull(act_grad.astype(jnp.float32))[0].astype(jnp.bfloat16)
    )
    grad_full = mixed_grad.astype(jnp.float32)
    upper = mix[levels] * grad_full
    mix_rows = [None] * (levels + 1)
    mix_rows[levels] = jnp.sum(grad_full * stored[levels].astype(jnp.float32), axis=0)
    theta = jnp.zeros((width,), jnp.float32)
    phi = jnp.zeros((width,), jnp.float32)
    carried = stored[0]
    for level in reversed(range(levels)):
        dist = 2**level
        plain = stored[level].astype(jnp.float32)
        shifted = taps[level].astype(jnp.float32)
        along = mix[level] * grad_full
        mix_rows[level] = jnp.sum(grad_full * (cos_d * plain + sin_d * shifted), axis=0)
        theta = theta + jnp.sum(upper * (cos_a * shifted - sin_a * plain), axis=0)
        phi = phi + jnp.sum(along * (cos_d * shifted - sin_d * plain), axis=0)
        sent = lax.optimization_barrier(
            (masks[level] * (sin_a * upper + sin_d * along)).astype(jnp.bfloat16)
        )
        if dist < rows:
            after = from_behind(sent[:dist], "seq", -1)
            back = jnp.concatenate([sent[dist:], after], axis=0)
        else:
            back = from_behind(sent, "seq", -(dist // rows))
        carried = lax.optimization_barrier(
            (cos_a * upper + cos_d * along + back.astype(jnp.float32)).astype(jnp.bfloat16)
        )
        upper = carried.astype(jnp.float32)
    angle_all, mix_all = lax.psum((jnp.stack([theta, phi]), jnp.stack(mix_rows)), ("stream", "seq"))
    weight_rows = lax.psum_scatter(
        lax.dot_general(
            act, local_cot, (((0,), (0,)), ((), ())), preferred_element_type=jnp.float32
        ),
        "seq",
        scatter_dimension=0,
        tiled=True,
    )
    weight_rows = lax.psum(weight_rows, "stream")
    return (output[None], carried[None], weight_rows * factor, angle_all * factor, mix_all * factor)


def solution(mesh):
    in_specs = (
        P("stream", "seq", None),
        P("stream", "seq", None),
        P("stream", None),
        P(),
        P(),
        P(),
    )
    out_specs = (P("stream", "seq", None), P("stream", "seq", None), P("seq", None), P(), P())
    return jax.shard_map(body, mesh=mesh, in_specs=in_specs, out_specs=out_specs, check_vma=False)
```

profile of v0, /device:TPU:8, one launch (start us, length us, event | category | flops | bytes accessed | tf_op | source)
XLA Modules:
  0.0 812.0 jit_solution(9908100230172136991)
XLA Ops:
  17.4 3.6 collective-permute-start.1
  38.0 3.6 collective-permute-done.4
  44.5 4.3 collective-permute-done.5
  51.7 5.8 collective-permute-done.6
  60.6 8.6 %collective-permute-done.7 = bf16[128,2048]{1,0:T(8,128)(2,1)S(1)} collective-permute-done((bf16[128,2048]{1,0:T(8,128)(2,1)S(1)}, bf16[128,2048]{1,0:T(8,128)(2,1)S(1)}, u32[]{:S(2)}, u32[]{:S(2)}) %collective-permute-start.7) | collective-permute-done | bytes 524320 | tf_op jit(solution)/shard_map/ppermute | solution.py:10
  73.6 11.4 %collective-permute-done.8 = bf16[128,2048]{1,0:T(8,128)(2,1)S(1)} collective-permute-done((bf16[128,2048]{1,0:T(8,128)(2,1)S(1)}, bf16[128,2048]{1,0:T(8,128)(2,1)S(1)}, u32[]{:S(2)}, u32[]{:S(2)}) %collective-permute-start.8) | collective-permute-done | bytes 524320 | tf_op jit(solution)/shard_map/ppermute | solution.py:10
  86.0 15.0 %collective-permute-start.9 = (bf16[128,2048]{1,0:T(8,128)(2,1)S(1)}, bf16[128,2048]{1,0:T(8,128)(2,1)S(1)}, u32[]{:S(2)}, u32[]{:S(2)}) collective-permute-start(bf16[128,2048]{1,0:T(8,128)(2,1)S(1)} %fusion.250), channel_id=1, source_target_pairs={{0,4},{1,5},{2,6},{3,7},{4,8},{5,9},{6,10},{7,11},{8,12},{9,13},{1... | collective-permute-start | bytes 1572872 | tf_op jit(solution)/shard_map/ppermute | solution.py:10
  101.0 7.5 collective-permute-done.9
  109.4 4.3 collective-permute-start.10
  113.8 6.6 collective-permute-done.10
  121.4 14.6 %collective-permute-start.11 = (bf16[128,2048]{1,0:T(8,128)(2,1)S(1)}, bf16[128,2048]{1,0:T(8,128)(2,1)S(1)}, u32[]{:S(2)}, u32[]{:S(2)}) collective-permute-start(bf16[128,2048]{1,0:T(8,128)(2,1)S(1)} %fusion.254), channel_id=1, source_target_pairs={{0,16},{1,17},{2,18},{3,19},{4,20},{5,21},{6,22},{7,23},{8,24},{9,... | collective-permute-start | bytes 1572872 | tf_op jit(solution)/shard_map/ppermute | solution.py:10
  136.0 8.1 collective-permute-done.11
  145.0 31.3 %collective-permute-start.12 = (bf16[128,2048]{1,0:T(8,128)(2,1)S(1)}, bf16[128,2048]{1,0:T(8,128)(2,1)S(1)}, u32[]{:S(2)}, u32[]{:S(2)}) collective-permute-start(bf16[128,2048]{1,0:T(8,128)(2,1)S(1)} %fusion.256), channel_id=1, source_target_pairs={{0,32},{1,33},{2,34},{3,35},{4,36},{5,37},{6,38},{7,39},{8,40},{9,... | collective-permute-start | bytes 1572872 | tf_op jit(solution)/shard_map/ppermute | solution.py:10
  179.5 7.8 collective-permute-done.12
  188.4 7.4 fusion.97
  197.1 8.1 %fusion.288 = f32[2048,2048]{1,0:T(8,128)} fusion(bf16[1,128,2048]{2,1,0:T(8,128)(2,1)S(1)} %copy-done, f32[128,2048]{1,0:T(8,128)S(1)} %get-tuple-element.55), kind=kOutput, calls=%fused_computation.471 | convolution fusion | flops 1076101120 | bytes 18350080 | tf_op jit(solution)/shard_map/dot_general | solution.py:108
  208.0 19.3 %collective-permute-done.13 = bf16[128,2048]{1,0:T(8,128)(2,1)S(1)} collective-permute-done((bf16[128,2048]{1,0:T(8,128)(2,1)S(1)}, bf16[128,2048]{1,0:T(8,128)(2,1)S(1)}, u32[]{:S(2)}, u32[]{:S(2)}) %collective-permute-start.13) | collective-permute-done | bytes 524320 | tf_op jit(solution)/shard_map/ppermute | solution.py:10
  230.6 26.2 %collective-permute-done.14 = bf16[128,2048]{1,0:T(8,128)(2,1)S(1)} collective-permute-done((bf16[128,2048]{1,0:T(8,128)(2,1)S(1)}, bf16[128,2048]{1,0:T(8,128)(2,1)S(1)}, u32[]{:S(2)}, u32[]{:S(2)}) %collective-permute-start.14) | collective-permute-done | bytes 524320 | tf_op jit(solution)/shard_map/ppermute | solution.py:10
  260.5 13.7 %collective-permute-done.15 = bf16[128,2048]{1,0:T(8,128)(2,1)S(1)} collective-permute-done((bf16[128,2048]{1,0:T(8,128)(2,1)S(1)}, bf16[128,2048]{1,0:T(8,128)(2,1)S(1)}, u32[]{:S(2)}, u32[]{:S(2)}) %collective-permute-start.15) | collective-permute-done | bytes 524320 | tf_op jit(solution)/shard_map/ppermute | solution.py:10
  279.7 19.8 %collective-permute-done.16 = bf16[128,2048]{1,0:T(8,128)(2,1)S(1)} collective-permute-done((bf16[128,2048]{1,0:T(8,128)(2,1)S(1)}, bf16[128,2048]{1,0:T(8,128)(2,1)S(1)}, u32[]{:S(2)}, u32[]{:S(2)}) %collective-permute-start.16) | collective-permute-done | bytes 524320 | tf_op jit(solution)/shard_map/ppermute | solution.py:10
  303.0 10.8 %collective-permute-start.17 = (bf16[128,2048]{1,0:T(8,128)(2,1)S(1)}, bf16[128,2048]{1,0:T(8,128)(2,1)S(1)}, u32[]{:S(2)}, u32[]{:S(2)}) collective-permute-start(bf16[128,2048]{1,0:T(8,128)(2,1)S(1)} %get-tuple-element.57), channel_id=1, source_target_pairs={{2,0},{3,1},{4,2},{5,3},{6,4},{7,5},{8,6},{9,7},{10,8},{11,9},{12,... | collective-permute-start | bytes 1572872 | tf_op jit(solution)/shard_map/ppermute | solution.py:10
  313.9 22.7 %collective-permute-done.17 = bf16[128,2048]{1,0:T(8,128)(2,1)S(1)} collective-permute-done((bf16[128,2048]{1,0:T(8,128)(2,1)S(1)}, bf16[128,2048]{1,0:T(8,128)(2,1)S(1)}, u32[]{:S(2)}, u32[]{:S(2)}) %collective-permute-start.17) | collective-permute-done | bytes 524320 | tf_op jit(solution)/shard_map/ppermute | solution.py:10
  341.9 6.7 collective-permute-done.18
  351.2 4.2 collective-permute-start.19
  355.4 3.9 collective-permute-done.19
  361.8 4.2 collective-permute-start.20
  366.1 5.5 collective-permute-done.20
  376.9 5.1 collective-permute-done.21
  386.0 3.6 collective-permute-done.22
  408.9 101.6 %psum.22 = f32[2,2048]{1,0:T(2,128)S(1)} all-reduce(f32[2,2048]{1,0:T(2,128)S(1)} %pad_maximum_fusion.7), channel_id=1, replica_groups=mesh['stream'=4,'seq'=64] {'stream','seq'}, use_global_device_ids=true, to_apply=%region_30.31 | all-reduce | flops 4096 | bytes 32768 | tf_op jit(solution)/shard_map/psum | solution.py:106
  514.0 243.3 %all-reduce.5.cloned.1.call-done = f32[14,2048]{1,0:T(8,128)} async-done(((f32[14,2048]{1,0:T(8,128)}), f32[14,2048]{1,0:T(8,128)}) %all-reduce.5.cloned.1.call-update) | async-done | bytes 114704 | tf_op jit(solution)/shard_map/psum | solution.py:106
  758.8 43.9 %all-reduce.3.cloned.1.call-done = f32[32,2048]{1,0:T(8,128)} async-done(((f32[32,2048]{1,0:T(8,128)}), f32[32,2048]{1,0:T(8,128)}) %all-reduce.3.cloned.1.call-update) | async-done | bytes 262160 | tf_op jit(solution)/shard_map/psum | solution.py:115
  (318 shorter events, 111.6 us)
Async XLA Ops:
  8.0 168.4 %copy-start = (bf16[1,128,2048]{2,1,0:T(8,128)(2,1)S(1)}, bf16[1,128,2048]{2,1,0:T(8,128)(2,1)}, u32[]{:S(2)}) copy-start(bf16[1,128,2048]{2,1,0:T(8,128)(2,1)} %param.7) | copy-start | bytes 1572868
  8.0 505.9 %reduce-scatter.2.cloned.1.call-start = ((), (), s32[]{:S(2)}) async-start(), calls=%async_computation.1 | async-start | bytes 17039360 | tf_op jit(solution)/shard_map/reduce_scatter | solution.py:107
  8.9 7.1 collective-permute-start
  17.4 5.1 collective-permute-start.1
  23.6 5.1 collective-permute-start.2
  28.6 159.6 %copy-start.65 = (bf16[4,2048]{1,0:T(4,128)(2,1)}, bf16[4,2048]{1,0:T(4,128)(2,1)S(1)}, u32[]{:S(2)}) copy-start(bf16[4,2048]{1,0:T(4,128)(2,1)S(1)} %collective-permute-done.2) | copy-start | bytes 49156
  29.7 5.2 collective-permute-start.3
  31.6 156.6 %copy-start.22 = (bf16[120,2048]{1,0:T(8,128)(2,1)}, bf16[120,2048]{1,0:T(8,128)(2,1)S(1)}, u32[]{:S(2)}) copy-start(bf16[120,2048]{1,0:T(8,128)(2,1)S(1)} %slice.205) | copy-start | bytes 1474564
  35.9 5.7 collective-permute-start.4
  42.6 6.3 collective-permute-start.5
  49.8 7.7 collective-permute-start.6
  58.5 10.6 %collective-permute-start.7 = (bf16[128,2048]{1,0:T(8,128)(2,1)S(1)}, bf16[128,2048]{1,0:T(8,128)(2,1)S(1)}, u32[]{:S(2)}, u32[]{:S(2)}) collective-permute-start(bf16[128,2048]{1,0:T(8,128)(2,1)S(1)} %fusion.246), channel_id=1, source_target_pairs={{0,1},{1,2},{2,3},{3,4},{4,5},{5,6},{6,7},{7,8},{8,9},{9,10},{10,1... | collective-permute-start | bytes 1572872 | tf_op jit(solution)/shard_map/ppermute | solution.py:10
  70.1 14.9 %collective-permute-start.8 = (bf16[128,2048]{1,0:T(8,128)(2,1)S(1)}, bf16[128,2048]{1,0:T(8,128)(2,1)S(1)}, u32[]{:S(2)}, u32[]{:S(2)}) collective-permute-start(bf16[128,2048]{1,0:T(8,128)(2,1)S(1)} %fusion.248), channel_id=1, source_target_pairs={{0,2},{1,3},{2,4},{3,5},{4,6},{5,7},{6,8},{7,9},{8,10},{9,11},{10,... | collective-permute-start | bytes 1572872 | tf_op jit(solution)/shard_map/ppermute | solution.py:10
  86.0 22.5 %collective-permute-start.9 = (bf16[128,2048]{1,0:T(8,128)(2,1)S(1)}, bf16[128,2048]{1,0:T(8,128)(2,1)S(1)}, u32[]{:S(2)}, u32[]{:S(2)}) collective-permute-start(bf16[128,2048]{1,0:T(8,128)(2,1)S(1)} %fusion.250), channel_id=1, source_target_pairs={{0,4},{1,5},{2,6},{3,7},{4,8},{5,9},{6,10},{7,11},{8,12},{9,13},{1... | collective-permute-start | bytes 1572872 | tf_op jit(solution)/shard_map/ppermute | solution.py:10
  109.4 11.0 %collective-permute-start.10 = (bf16[128,2048]{1,0:T(8,128)(2,1)S(1)}, bf16[128,2048]{1,0:T(8,128)(2,1)S(1)}, u32[]{:S(2)}, u32[]{:S(2)}) collective-permute-start(bf16[128,2048]{1,0:T(8,128)(2,1)S(1)} %fusion.252), channel_id=1, source_target_pairs={{0,8},{1,9},{2,10},{3,11},{4,12},{5,13},{6,14},{7,15},{8,16},{9,17... | collective-permute-start | bytes 1572872 | tf_op jit(solution)/shard_map/ppermute | solution.py:10
  121.4 22.7 %collective-permute-start.11 = (bf16[128,2048]{1,0:T(8,128)(2,1)S(1)}, bf16[128,2048]{1,0:T(8,128)(2,1)S(1)}, u32[]{:S(2)}, u32[]{:S(2)}) collective-permute-start(bf16[128,2048]{1,0:T(8,128)(2,1)S(1)} %fusion.254), channel_id=1, source_target_pairs={{0,16},{1,17},{2,18},{3,19},{4,20},{5,21},{6,22},{7,23},{8,24},{9,... | collective-permute-start | bytes 1572872 | tf_op jit(solution)/shard_map/ppermute | solution.py:10
  145.0 42.4 %collective-permute-start.12 = (bf16[128,2048]{1,0:T(8,128)(2,1)S(1)}, bf16[128,2048]{1,0:T(8,128)(2,1)S(1)}, u32[]{:S(2)}, u32[]{:S(2)}) collective-permute-start(bf16[128,2048]{1,0:T(8,128)(2,1)S(1)} %fusion.256), channel_id=1, source_target_pairs={{0,32},{1,33},{2,34},{3,35},{4,36},{5,37},{6,38},{7,39},{8,40},{9,... | collective-permute-start | bytes 1572872 | tf_op jit(solution)/shard_map/ppermute | solution.py:10
  205.2 552.0 %all-reduce.5.cloned.1.call-start = ((), (), s32[]{:S(2)}) async-start(), calls=%async_computation.3 | async-start | bytes 262144 | tf_op jit(solution)/shard_map/psum | solution.py:106
  206.6 20.8 %collective-permute-start.13 = (bf16[128,2048]{1,0:T(8,128)(2,1)S(1)}, bf16[128,2048]{1,0:T(8,128)(2,1)S(1)}, u32[]{:S(2)}, u32[]{:S(2)}) collective-permute-start(bf16[128,2048]{1,0:T(8,128)(2,1)S(1)} %fusion.189), channel_id=1, source_target_pairs={{32,0},{33,1},{34,2},{35,3},{36,4},{37,5},{38,6},{39,7},{40,8},{41... | collective-permute-start | bytes 1572872 | tf_op jit(solution)/shard_map/ppermute | solution.py:10
  229.3 27.5 %collective-permute-start.14 = (bf16[128,2048]{1,0:T(8,128)(2,1)S(1)}, bf16[128,2048]{1,0:T(8,128)(2,1)S(1)}, u32[]{:S(2)}, u32[]{:S(2)}) collective-permute-start(bf16[128,2048]{1,0:T(8,128)(2,1)S(1)} %fusion.182), channel_id=1, source_target_pairs={{16,0},{17,1},{18,2},{19,3},{20,4},{21,5},{22,6},{23,7},{24,8},{25... | collective-permute-start | bytes 1572872 | tf_op jit(solution)/shard_map/ppermute | solution.py:10
  259.1 15.1 %collective-permute-start.15 = (bf16[128,2048]{1,0:T(8,128)(2,1)S(1)}, bf16[128,2048]{1,0:T(8,128)(2,1)S(1)}, u32[]{:S(2)}, u32[]{:S(2)}) collective-permute-start(bf16[128,2048]{1,0:T(8,128)(2,1)S(1)} %fusion.175), channel_id=1, source_target_pairs={{8,0},{9,1},{10,2},{11,3},{12,4},{13,5},{14,6},{15,7},{16,8},{17,9... | collective-permute-start | bytes 1572872 | tf_op jit(solution)/shard_map/ppermute | solution.py:10
  278.5 21.1 %collective-permute-start.16 = (bf16[128,2048]{1,0:T(8,128)(2,1)S(1)}, bf16[128,2048]{1,0:T(8,128)(2,1)S(1)}, u32[]{:S(2)}, u32[]{:S(2)}) collective-permute-start(bf16[128,2048]{1,0:T(8,128)(2,1)S(1)} %get-tuple-element.56), channel_id=1, source_target_pairs={{4,0},{5,1},{6,2},{7,3},{8,4},{9,5},{10,6},{11,7},{12,8},{13,9},{1... | collective-permute-start | bytes 1572872 | tf_op jit(solution)/shard_map/ppermute | solution.py:10
  303.0 33.5 %collective-permute-start.17 = (bf16[128,2048]{1,0:T(8,128)(2,1)S(1)}, bf16[128,2048]{1,0:T(8,128)(2,1)S(1)}, u32[]{:S(2)}, u32[]{:S(2)}) collective-permute-start(bf16[128,2048]{1,0:T(8,128)(2,1)S(1)} %get-tuple-element.57), channel_id=1, source_target_pairs={{2,0},{3,1},{4,2},{5,3},{6,4},{7,5},{8,6},{9,7},{10,8},{11,9},{12,... | collective-permute-start | bytes 1572872 | tf_op jit(solution)/shard_map/ppermute | solution.py:10
  340.0 8.6 %collective-permute-start.18 = (bf16[128,2048]{1,0:T(8,128)(2,1)S(1)}, bf16[128,2048]{1,0:T(8,128)(2,1)S(1)}, u32[]{:S(2)}, u32[]{:S(2)}) collective-permute-start(bf16[128,2048]{1,0:T(8,128)(2,1)S(1)} %get-tuple-element.58), channel_id=1, source_target_pairs={{1,0},{2,1},{3,2},{4,3},{5,4},{6,5},{7,6},{8,7},{9,8},{10,9},{11,1... | collective-permute-start | bytes 1572872 | tf_op jit(solution)/shard_map/ppermute | solution.py:10
  351.2 8.1 collective-permute-start.19
  361.8 9.7 %collective-permute-start.20 = (bf16[32,2048]{1,0:T(8,128)(2,1)S(1)}, bf16[32,2048]{1,0:T(8,128)(2,1)S(1)}, u32[]{:S(2)}, u32[]{:S(2)}) collective-permute-start(bf16[32,2048]{1,0:T(8,128)(2,1)S(1)} %slice.215), channel_id=1, source_target_pairs={{1,0},{2,1},{3,2},{4,3},{5,4},{6,5},{7,6},{8,7},{9,8},{10,9},{11,1... | collective-permute-start | bytes 393224 | tf_op jit(solution)/shard_map/ppermute | solution.py:10
  373.5 8.6 %collective-permute-start.21 = (bf16[16,2048]{1,0:T(8,128)(2,1)S(1)}, bf16[16,2048]{1,0:T(8,128)(2,1)S(1)}, u32[]{:S(2)}, u32[]{:S(2)}) collective-permute-start(bf16[16,2048]{1,0:T(8,128)(2,1)S(1)} %slice.217), channel_id=1, source_target_pairs={{1,0},{2,1},{3,2},{4,3},{5,4},{6,5},{7,6},{8,7},{9,8},{10,9},{11,1... | collective-permute-start | bytes 196616 | tf_op jit(solution)/shard_map/ppermute | solution.py:10
  384.0 5.5 collective-permute-start.22
  391.8 5.2 collective-permute-start.23
  399.2 5.2 collective-permute-start.24
  406.6 106.2 %collective-permute-start.25 = (bf16[1,2048]{1,0:T(2,128)(2,1)S(1)}, bf16[1,2048]{1,0:T(2,128)(2,1)S(1)}, u32[]{:S(2)}, u32[]{:S(2)}) collective-permute-start(bf16[1,2048]{1,0:T(2,128)(2,1)S(1)} %slice.225), channel_id=1, source_target_pairs={{1,0},{2,1},{3,2},{4,3},{5,4},{6,5},{7,6},{8,7},{9,8},{10,9},{11,1... | collective-permute-start | bytes 12296 | tf_op jit(solution)/shard_map/ppermute | solution.py:10
  512.7 289.9 %all-reduce.3.cloned.1.call-start = ((), (), s32[]{:S(2)}) async-start(), calls=%async_computation.2 | async-start | bytes 524288 | tf_op jit(solution)/shard_map/psum | solution.py:115
  (100 other events, 6889.8 us)
Sparse Core Ops, SparseCore 0:
  205.4 223.6 reduce-scatter.1
Sparse Core Ops, SparseCore 1:
  512.8 244.4 all-reduce.4
  759.4 43.2 all-reduce.2
where the time goes:
time: 819 us; the launch traced here: 812 us
  waiting for transfers between devices  489 us (60%)
  starting transfers between devices  124 us (15%)
  blocking collectives  102 us (12%)
  other arithmetic  58.4 us (7%)
  between operations  17.8 us (2%)
  matrix products  13.3 us (2%)
    psum x1, waiting for transfers between devices, body(): lax.psum((jnp.stack([theta, phi]), jnp.stack(mix_rows)), ('stream', 'seq'))  243 us
    ppermute x26, waiting for transfers between devices, from_behind(): return lax.ppermute(block, axis, route)  202 us
    ppermute x26, starting transfers between devices, from_behind(): return lax.ppermute(block, axis, route)  124 us
    psum x1, blocking collectives, body(): lax.psum((jnp.stack([theta, phi]), jnp.stack(mix_rows)), ('stream', 'seq'))  102 us
    psum x1, waiting for transfers between devices, body(): weight_rows = lax.psum(weight_rows, 'stream')  43.9 us
    reduce_sum x10, other arithmetic, body(): jnp.sum(grad_full * (cos_d * plain + sin_d * shifted), axis=0)  22.1 us
  transfers between devices with their start and end apart: 29, of which 26 were waited for; matrix products, arithmetic and copies ran while one was open for 6% of the time, Pallas kernels for 0%

commit v1 on v0

--- a/solution.py
+++ b/solution.py
@@ -112,7 +112,7 @@
         scatter_dimension=0,
         tiled=True,
     )
-    weight_rows = lax.psum(weight_rows, "stream")
+    weight_rows = jnp.sum(lax.all_gather(weight_rows, axis_name="stream"), axis=0)
     return (output[None], carried[None], weight_rows * factor, angle_all * factor, mix_all * factor)
 
 

time: 819 us -> 701 us (0.86)
  waiting for transfers between devices: 489 us -> 389 us
  blocking collectives: 102 us -> 83.9 us
    psum x1, waiting for transfers between devices: 243 us -> 168 us  [body(): lax.psum((jnp.stack([theta, phi]), jnp.stack(mix_rows)), ('stream', 'seq'))]
    psum x1 -> x0, waiting for transfers between devices: 43.9 us -> none  [body(): weight_rows = lax.psum(weight_rows, 'stream')]
    reduce_scatter x1, waiting for transfers between devices: 0.01 us -> 18.9 us  [body(): lax.psum_scatter(lax.dot_general(act, local_cot, (((0,), (0,)), ((), ()))...]
    psum x1, blocking collectives: 102 us -> 83.9 us  [body(): lax.psum((jnp.stack([theta, phi]), jnp.stack(mix_rows)), ('stream', 'seq'))]
  transfers between devices with their start and end apart: 29 -> 29, of which waited for: 26 -> 26; matrix products, arithmetic and copies ran while one was open for 6% -> 7% of each run, Pallas kernels for 0% -> 0%
where the time goes in v1:
time: 701 us; the launch traced here: 695 us
  waiting for transfers between devices  389 us (55%)
  starting transfers between devices  124 us (18%)
  blocking collectives  83.9 us (12%)
  other arithmetic  58.9 us (8%)
  between operations  18.1 us (3%)
  matrix products  13.4 us (2%)
  local copies, waits for them, and re-layouts  7.5 us (1%)
    ppermute x26, waiting for transfers between devices, from_behind(): return lax.ppermute(block, axis, route)  201 us
    psum x1, waiting for transfers between devices, body(): lax.psum((jnp.stack([theta, phi]), jnp.stack(mix_rows)), ('stream', 'seq'))  168 us
    ppermute x26, starting transfers between devices, from_behind(): return lax.ppermute(block, axis, route)  124 us
    psum x1, blocking collectives, body(): lax.psum((jnp.stack([theta, phi]), jnp.stack(mix_rows)), ('stream', 'seq'))  83.9 us
    reduce_sum x10, other arithmetic, body(): jnp.sum(grad_full * (cos_d * plain + sin_d * shifted), axis=0)  22.3 us
    reduce_scatter x1, waiting for transfers between devices, body(): lax.psum_scatter(lax.dot_general(act, local_cot, (((0,), (0,)), ((), ()))...  18.9 us
  transfers between devices with their start and end apart: 29, of which 26 were waited for; matrix products, arithmetic and copies ran while one was open for 7% of the time, Pallas kernels for 0%

profile of v1, /device:TPU:8, one launch (start us, length us, event | category | flops | bytes accessed | tf_op | source)
XLA Modules:
  0.0 694.6 jit_solution(1018018424241193688)
XLA Ops:
  17.4 3.6 collective-permute-start.1
  38.0 3.6 collective-permute-done.4
  44.6 4.3 collective-permute-done.5
  51.8 5.8 collective-permute-done.6
  60.6 8.6 %collective-permute-done.7 = bf16[128,2048]{1,0:T(8,128)(2,1)S(1)} collective-permute-done((bf16[128,2048]{1,0:T(8,128)(2,1)S(1)}, bf16[128,2048]{1,0:T(8,128)(2,1)S(1)}, u32[]{:S(2)}, u32[]{:S(2)}) %collective-permute-start.7) | collective-permute-done | bytes 524320 | tf_op jit(solution)/shard_map/ppermute | solution.py:10
  73.7 11.4 %collective-permute-done.8 = bf16[128,2048]{1,0:T(8,128)(2,1)S(1)} collective-permute-done((bf16[128,2048]{1,0:T(8,128)(2,1)S(1)}, bf16[128,2048]{1,0:T(8,128)(2,1)S(1)}, u32[]{:S(2)}, u32[]{:S(2)}) %collective-permute-start.8) | collective-permute-done | bytes 524320 | tf_op jit(solution)/shard_map/ppermute | solution.py:10
  86.0 15.1 %collective-permute-start.9 = (bf16[128,2048]{1,0:T(8,128)(2,1)S(1)}, bf16[128,2048]{1,0:T(8,128)(2,1)S(1)}, u32[]{:S(2)}, u32[]{:S(2)}) collective-permute-start(bf16[128,2048]{1,0:T(8,128)(2,1)S(1)} %fusion.250), channel_id=1, source_target_pairs={{0,4},{1,5},{2,6},{3,7},{4,8},{5,9},{6,10},{7,11},{8,12},{9,13},{1... | collective-permute-start | bytes 1572872 | tf_op jit(solution)/shard_map/ppermute | solution.py:10
  101.1 7.4 %collective-permute-done.9 = bf16[128,2048]{1,0:T(8,128)(2,1)S(1)} collective-permute-done((bf16[128,2048]{1,0:T(8,128)(2,1)S(1)}, bf16[128,2048]{1,0:T(8,128)(2,1)S(1)}, u32[]{:S(2)}, u32[]{:S(2)}) %collective-permute-start.9) | collective-permute-done | bytes 524320 | tf_op jit(solution)/shard_map/ppermute | solution.py:10
  109.5 4.4 collective-permute-start.10
  113.9 6.6 collective-permute-done.10
  121.5 14.6 %collective-permute-start.11 = (bf16[128,2048]{1,0:T(8,128)(2,1)S(1)}, bf16[128,2048]{1,0:T(8,128)(2,1)S(1)}, u32[]{:S(2)}, u32[]{:S(2)}) collective-permute-start(bf16[128,2048]{1,0:T(8,128)(2,1)S(1)} %fusion.254), channel_id=1, source_target_pairs={{0,16},{1,17},{2,18},{3,19},{4,20},{5,21},{6,22},{7,23},{8,24},{9,... | collective-permute-start | bytes 1572872 | tf_op jit(solution)/shard_map/ppermute | solution.py:10
  136.0 8.1 %collective-permute-done.11 = bf16[128,2048]{1,0:T(8,128)(2,1)S(1)} collective-permute-done((bf16[128,2048]{1,0:T(8,128)(2,1)S(1)}, bf16[128,2048]{1,0:T(8,128)(2,1)S(1)}, u32[]{:S(2)}, u32[]{:S(2)}) %collective-permute-start.11) | collective-permute-done | bytes 524320 | tf_op jit(solution)/shard_map/ppermute | solution.py:10
  145.0 31.3 %collective-permute-start.12 = (bf16[128,2048]{1,0:T(8,128)(2,1)S(1)}, bf16[128,2048]{1,0:T(8,128)(2,1)S(1)}, u32[]{:S(2)}, u32[]{:S(2)}) collective-permute-start(bf16[128,2048]{1,0:T(8,128)(2,1)S(1)} %fusion.256), channel_id=1, source_target_pairs={{0,32},{1,33},{2,34},{3,35},{4,36},{5,37},{6,38},{7,39},{8,40},{9,... | collective-permute-start | bytes 1572872 | tf_op jit(solution)/shard_map/ppermute | solution.py:10
  179.6 7.8 %collective-permute-done.12 = bf16[128,2048]{1,0:T(8,128)(2,1)S(1)} collective-permute-done((bf16[128,2048]{1,0:T(8,128)(2,1)S(1)}, bf16[128,2048]{1,0:T(8,128)(2,1)S(1)}, u32[]{:S(2)}, u32[]{:S(2)}) %collective-permute-start.12) | collective-permute-done | bytes 524320 | tf_op jit(solution)/shard_map/ppermute | solution.py:10
  188.4 7.4 %fusion.97 = (bf16[128,2048]{1,0:T(8,128)(2,1)S(1)}, f32[128,2048]{1,0:T(8,128)S(1)}) fusion(bf16[128,2048]{1,0:T(8,128)(2,1)S(1)} %convolution_convert_fusion, bf16[128,2048]{1,0:T(8,128)(2,1)S(1)} %fusion.258, f32[2048]{0:T(1024)S(1)} %bitcast.174, f32[128]{0:T(128)} %get-tuple-element.88, bf16[128,2048]{1,0:T(8,128)(2,1)S(1)} %collective-permute-done.12, ...), kind=kLoop, calls=%fused_computation.259 | loop fusion | flops 38797312 | bytes 16390656 | tf_op jit(solution)/shard_map/convert_element_type | solution.py:77
  197.0 8.2 %fusion.288 = f32[2048,2048]{1,0:T(8,128)} fusion(bf16[1,128,2048]{2,1,0:T(8,128)(2,1)S(1)} %copy-done, f32[128,2048]{1,0:T(8,128)S(1)} %get-tuple-element.55), kind=kOutput, calls=%fused_computation.471 | convolution fusion | flops 1076101120 | bytes 18350080 | tf_op jit(solution)/shard_map/dot_general | solution.py:108
  208.0 19.3 %collective-permute-done.13 = bf16[128,2048]{1,0:T(8,128)(2,1)S(1)} collective-permute-done((bf16[128,2048]{1,0:T(8,128)(2,1)S(1)}, bf16[128,2048]{1,0:T(8,128)(2,1)S(1)}, u32[]{:S(2)}, u32[]{:S(2)}) %collective-permute-start.13) | collective-permute-done | bytes 524320 | tf_op jit(solution)/shard_map/ppermute | solution.py:10
  230.6 26.2 %collective-permute-done.14 = bf16[128,2048]{1,0:T(8,128)(2,1)S(1)} collective-permute-done((bf16[128,2048]{1,0:T(8,128)(2,1)S(1)}, bf16[128,2048]{1,0:T(8,128)(2,1)S(1)}, u32[]{:S(2)}, u32[]{:S(2)}) %collective-permute-start.14) | collective-permute-done | bytes 524320 | tf_op jit(solution)/shard_map/ppermute | solution.py:10
  260.5 13.7 %collective-permute-done.15 = bf16[128,2048]{1,0:T(8,128)(2,1)S(1)} collective-permute-done((bf16[128,2048]{1,0:T(8,128)(2,1)S(1)}, bf16[128,2048]{1,0:T(8,128)(2,1)S(1)}, u32[]{:S(2)}, u32[]{:S(2)}) %collective-permute-start.15) | collective-permute-done | bytes 524320 | tf_op jit(solution)/shard_map/ppermute | solution.py:10
  279.7 19.8 %collective-permute-done.16 = bf16[128,2048]{1,0:T(8,128)(2,1)S(1)} collective-permute-done((bf16[128,2048]{1,0:T(8,128)(2,1)S(1)}, bf16[128,2048]{1,0:T(8,128)(2,1)S(1)}, u32[]{:S(2)}, u32[]{:S(2)}) %collective-permute-start.16) | collective-permute-done | bytes 524320 | tf_op jit(solution)/shard_map/ppermute | solution.py:10
  303.0 10.8 %collective-permute-start.17 = (bf16[128,2048]{1,0:T(8,128)(2,1)S(1)}, bf16[128,2048]{1,0:T(8,128)(2,1)S(1)}, u32[]{:S(2)}, u32[]{:S(2)}) collective-permute-start(bf16[128,2048]{1,0:T(8,128)(2,1)S(1)} %get-tuple-element.57), channel_id=1, source_target_pairs={{2,0},{3,1},{4,2},{5,3},{6,4},{7,5},{8,6},{9,7},{10,8},{11,9},{12,... | collective-permute-start | bytes 1572872 | tf_op jit(solution)/shard_map/ppermute | solution.py:10
  313.8 22.7 %collective-permute-done.17 = bf16[128,2048]{1,0:T(8,128)(2,1)S(1)} collective-permute-done((bf16[128,2048]{1,0:T(8,128)(2,1)S(1)}, bf16[128,2048]{1,0:T(8,128)(2,1)S(1)}, u32[]{:S(2)}, u32[]{:S(2)}) %collective-permute-start.17) | collective-permute-done | bytes 524320 | tf_op jit(solution)/shard_map/ppermute | solution.py:10
  341.9 6.7 collective-permute-done.18
  351.2 4.2 collective-permute-start.19
  355.4 3.9 collective-permute-done.19
  361.8 4.2 collective-permute-start.20
  366.1 4.7 collective-permute-done.20
  376.3 4.7 collective-permute-done.21
  384.9 3.6 collective-permute-done.22
  410.1 18.9 %reduce-scatter.2.cloned.1.call-done = f32[32,2048]{1,0:T(8,128)} async-done(((f32[2048,2048]{1,0:T(8,128)}), f32[32,2048]{1,0:T(8,128)}) %reduce-scatter.2.cloned.1.call-update) | async-done | bytes 262160 | tf_op jit(solution)/shard_map/reduce_scatter | solution.py:107
  429.0 83.9 %psum.14 = f32[2,2048]{1,0:T(2,128)S(1)} all-reduce(f32[2,2048]{1,0:T(2,128)S(1)} %pad_maximum_fusion.7), channel_id=1, replica_groups=mesh['stream'=4,'seq'=64] {'stream','seq'}, use_global_device_ids=true, to_apply=%region_30.31 | all-reduce | flops 4096 | bytes 32768 | tf_op jit(solution)/shard_map/psum | solution.py:106
  514.8 168.4 %all-reduce.2.cloned.1.call-done = f32[14,2048]{1,0:T(8,128)} async-done(((f32[14,2048]{1,0:T(8,128)}), f32[14,2048]{1,0:T(8,128)}) %all-reduce.2.cloned.1.call-update) | async-done | bytes 114704 | tf_op jit(solution)/shard_map/psum | solution.py:106
  (351 shorter events, 112.5 us)
Async XLA Ops:
  8.0 168.3 %copy-start = (bf16[1,128,2048]{2,1,0:T(8,128)(2,1)S(1)}, bf16[1,128,2048]{2,1,0:T(8,128)(2,1)}, u32[]{:S(2)}) copy-start(bf16[1,128,2048]{2,1,0:T(8,128)(2,1)} %param.7) | copy-start | bytes 1572868
  8.0 421.0 %reduce-scatter.2.cloned.1.call-start = ((), (), s32[]{:S(2)}) async-start(), calls=%async_computation.1 | async-start | bytes 17039360 | tf_op jit(solution)/shard_map/reduce_scatter | solution.py:107
  8.9 7.1 %collective-permute-start = (bf16[1,2048]{1,0:T(2,128)(2,1)S(1)}, bf16[1,2048]{1,0:T(2,128)(2,1)S(1)}, u32[]{:S(2)}, u32[]{:S(2)}) collective-permute-start(bf16[1,2048]{1,0:T(2,128)(2,1)S(1)} %slice_bitcast_fusion.1), channel_id=1, source_target_pairs={{0,1},{1,2},{2,3},{3,4},{4,5},{5,6},{6,7},{7,8},{8,9},{9,10},{10,1... | collective-permute-start | bytes 12296 | tf_op jit(solution)/shard_map/ppermute | solution.py:10
  17.4 5.1 collective-permute-start.1
  23.5 5.1 collective-permute-start.2
  28.6 159.6 %copy-start.65 = (bf16[4,2048]{1,0:T(4,128)(2,1)}, bf16[4,2048]{1,0:T(4,128)(2,1)S(1)}, u32[]{:S(2)}) copy-start(bf16[4,2048]{1,0:T(4,128)(2,1)S(1)} %collective-permute-done.2) | copy-start | bytes 49156
  29.6 5.2 collective-permute-start.3
  31.5 156.7 %copy-start.22 = (bf16[120,2048]{1,0:T(8,128)(2,1)}, bf16[120,2048]{1,0:T(8,128)(2,1)S(1)}, u32[]{:S(2)}) copy-start(bf16[120,2048]{1,0:T(8,128)(2,1)S(1)} %slice.205) | copy-start | bytes 1474564
  35.9 5.7 collective-permute-start.4
  42.6 6.3 collective-permute-start.5
  49.8 7.7 %collective-permute-start.6 = (bf16[64,2048]{1,0:T(8,128)(2,1)S(1)}, bf16[64,2048]{1,0:T(8,128)(2,1)S(1)}, u32[]{:S(2)}, u32[]{:S(2)}) collective-permute-start(bf16[64,2048]{1,0:T(8,128)(2,1)S(1)} %get-tuple-element.68), channel_id=1, source_target_pairs={{0,1},{1,2},{2,3},{3,4},{4,5},{5,6},{6,7},{7,8},{8,9},{9,10},{10,1... | collective-permute-start | bytes 786440 | tf_op jit(solution)/shard_map/ppermute | solution.py:10
  58.6 10.6 %collective-permute-start.7 = (bf16[128,2048]{1,0:T(8,128)(2,1)S(1)}, bf16[128,2048]{1,0:T(8,128)(2,1)S(1)}, u32[]{:S(2)}, u32[]{:S(2)}) collective-permute-start(bf16[128,2048]{1,0:T(8,128)(2,1)S(1)} %fusion.246), channel_id=1, source_target_pairs={{0,1},{1,2},{2,3},{3,4},{4,5},{5,6},{6,7},{7,8},{8,9},{9,10},{10,1... | collective-permute-start | bytes 1572872 | tf_op jit(solution)/shard_map/ppermute | solution.py:10
  70.2 14.9 %collective-permute-start.8 = (bf16[128,2048]{1,0:T(8,128)(2,1)S(1)}, bf16[128,2048]{1,0:T(8,128)(2,1)S(1)}, u32[]{:S(2)}, u32[]{:S(2)}) collective-permute-start(bf16[128,2048]{1,0:T(8,128)(2,1)S(1)} %fusion.248), channel_id=1, source_target_pairs={{0,2},{1,3},{2,4},{3,5},{4,6},{5,7},{6,8},{7,9},{8,10},{9,11},{10,... | collective-permute-start | bytes 1572872 | tf_op jit(solution)/shard_map/ppermute | solution.py:10
  86.0 22.5 %collective-permute-start.9 = (bf16[128,2048]{1,0:T(8,128)(2,1)S(1)}, bf16[128,2048]{1,0:T(8,128)(2,1)S(1)}, u32[]{:S(2)}, u32[]{:S(2)}) collective-permute-start(bf16[128,2048]{1,0:T(8,128)(2,1)S(1)} %fusion.250), channel_id=1, source_target_pairs={{0,4},{1,5},{2,6},{3,7},{4,8},{5,9},{6,10},{7,11},{8,12},{9,13},{1... | collective-permute-start | bytes 1572872 | tf_op jit(solution)/shard_map/ppermute | solution.py:10
  109.5 11.1 %collective-permute-start.10 = (bf16[128,2048]{1,0:T(8,128)(2,1)S(1)}, bf16[128,2048]{1,0:T(8,128)(2,1)S(1)}, u32[]{:S(2)}, u32[]{:S(2)}) collective-permute-start(bf16[128,2048]{1,0:T(8,128)(2,1)S(1)} %fusion.252), channel_id=1, source_target_pairs={{0,8},{1,9},{2,10},{3,11},{4,12},{5,13},{6,14},{7,15},{8,16},{9,17... | collective-permute-start | bytes 1572872 | tf_op jit(solution)/shard_map/ppermute | solution.py:10
  121.5 22.6 %collective-permute-start.11 = (bf16[128,2048]{1,0:T(8,128)(2,1)S(1)}, bf16[128,2048]{1,0:T(8,128)(2,1)S(1)}, u32[]{:S(2)}, u32[]{:S(2)}) collective-permute-start(bf16[128,2048]{1,0:T(8,128)(2,1)S(1)} %fusion.254), channel_id=1, source_target_pairs={{0,16},{1,17},{2,18},{3,19},{4,20},{5,21},{6,22},{7,23},{8,24},{9,... | collective-permute-start | bytes 1572872 | tf_op jit(solution)/shard_map/ppermute | solution.py:10
  145.0 42.4 %collective-permute-start.12 = (bf16[128,2048]{1,0:T(8,128)(2,1)S(1)}, bf16[128,2048]{1,0:T(8,128)(2,1)S(1)}, u32[]{:S(2)}, u32[]{:S(2)}) collective-permute-start(bf16[128,2048]{1,0:T(8,128)(2,1)S(1)} %fusion.256), channel_id=1, source_target_pairs={{0,32},{1,33},{2,34},{3,35},{4,36},{5,37},{6,38},{7,39},{8,40},{9,... | collective-permute-start | bytes 1572872 | tf_op jit(solution)/shard_map/ppermute | solution.py:10
  205.2 478.1 %all-reduce.2.cloned.1.call-start = ((), (), s32[]{:S(2)}) async-start(), calls=%async_computation.2 | async-start | bytes 262144 | tf_op jit(solution)/shard_map/psum | solution.py:106
  206.5 20.8 %collective-permute-start.13 = (bf16[128,2048]{1,0:T(8,128)(2,1)S(1)}, bf16[128,2048]{1,0:T(8,128)(2,1)S(1)}, u32[]{:S(2)}, u32[]{:S(2)}) collective-permute-start(bf16[128,2048]{1,0:T(8,128)(2,1)S(1)} %fusion.189), channel_id=1, source_target_pairs={{32,0},{33,1},{34,2},{35,3},{36,4},{37,5},{38,6},{39,7},{40,8},{41... | collective-permute-start | bytes 1572872 | tf_op jit(solution)/shard_map/ppermute | solution.py:10
  229.3 27.5 %collective-permute-start.14 = (bf16[128,2048]{1,0:T(8,128)(2,1)S(1)}, bf16[128,2048]{1,0:T(8,128)(2,1)S(1)}, u32[]{:S(2)}, u32[]{:S(2)}) collective-permute-start(bf16[128,2048]{1,0:T(8,128)(2,1)S(1)} %fusion.182), channel_id=1, source_target_pairs={{16,0},{17,1},{18,2},{19,3},{20,4},{21,5},{22,6},{23,7},{24,8},{25... | collective-permute-start | bytes 1572872 | tf_op jit(solution)/shard_map/ppermute | solution.py:10
  259.0 15.1 %collective-permute-start.15 = (bf16[128,2048]{1,0:T(8,128)(2,1)S(1)}, bf16[128,2048]{1,0:T(8,128)(2,1)S(1)}, u32[]{:S(2)}, u32[]{:S(2)}) collective-permute-start(bf16[128,2048]{1,0:T(8,128)(2,1)S(1)} %fusion.175), channel_id=1, source_target_pairs={{8,0},{9,1},{10,2},{11,3},{12,4},{13,5},{14,6},{15,7},{16,8},{17,9... | collective-permute-start | bytes 1572872 | tf_op jit(solution)/shard_map/ppermute | solution.py:10
  278.5 21.1 %collective-permute-start.16 = (bf16[128,2048]{1,0:T(8,128)(2,1)S(1)}, bf16[128,2048]{1,0:T(8,128)(2,1)S(1)}, u32[]{:S(2)}, u32[]{:S(2)}) collective-permute-start(bf16[128,2048]{1,0:T(8,128)(2,1)S(1)} %get-tuple-element.56), channel_id=1, source_target_pairs={{4,0},{5,1},{6,2},{7,3},{8,4},{9,5},{10,6},{11,7},{12,8},{13,9},{1... | collective-permute-start | bytes 1572872 | tf_op jit(solution)/shard_map/ppermute | solution.py:10
  303.0 33.5 %collective-permute-start.17 = (bf16[128,2048]{1,0:T(8,128)(2,1)S(1)}, bf16[128,2048]{1,0:T(8,128)(2,1)S(1)}, u32[]{:S(2)}, u32[]{:S(2)}) collective-permute-start(bf16[128,2048]{1,0:T(8,128)(2,1)S(1)} %get-tuple-element.57), channel_id=1, source_target_pairs={{2,0},{3,1},{4,2},{5,3},{6,4},{7,5},{8,6},{9,7},{10,8},{11,9},{12,... | collective-permute-start | bytes 1572872 | tf_op jit(solution)/shard_map/ppermute | solution.py:10
  339.9 8.6 %collective-permute-start.18 = (bf16[128,2048]{1,0:T(8,128)(2,1)S(1)}, bf16[128,2048]{1,0:T(8,128)(2,1)S(1)}, u32[]{:S(2)}, u32[]{:S(2)}) collective-permute-start(bf16[128,2048]{1,0:T(8,128)(2,1)S(1)} %get-tuple-element.58), channel_id=1, source_target_pairs={{1,0},{2,1},{3,2},{4,3},{5,4},{6,5},{7,6},{8,7},{9,8},{10,9},{11,1... | collective-permute-start | bytes 1572872 | tf_op jit(solution)/shard_map/ppermute | solution.py:10
  351.2 8.1 %collective-permute-start.19 = (bf16[64,2048]{1,0:T(8,128)(2,1)S(1)}, bf16[64,2048]{1,0:T(8,128)(2,1)S(1)}, u32[]{:S(2)}, u32[]{:S(2)}) collective-permute-start(bf16[64,2048]{1,0:T(8,128)(2,1)S(1)} %get-tuple-element.67), channel_id=1, source_target_pairs={{1,0},{2,1},{3,2},{4,3},{5,4},{6,5},{7,6},{8,7},{9,8},{10,9},{11,1... | collective-permute-start | bytes 786440 | tf_op jit(solution)/shard_map/ppermute | solution.py:10
  361.8 9.0 %collective-permute-start.20 = (bf16[32,2048]{1,0:T(8,128)(2,1)S(1)}, bf16[32,2048]{1,0:T(8,128)(2,1)S(1)}, u32[]{:S(2)}, u32[]{:S(2)}) collective-permute-start(bf16[32,2048]{1,0:T(8,128)(2,1)S(1)} %slice.215), channel_id=1, source_target_pairs={{1,0},{2,1},{3,2},{4,3},{5,4},{6,5},{7,6},{8,7},{9,8},{10,9},{11,1... | collective-permute-start | bytes 393224 | tf_op jit(solution)/shard_map/ppermute | solution.py:10
  372.8 8.2 %collective-permute-start.21 = (bf16[16,2048]{1,0:T(8,128)(2,1)S(1)}, bf16[16,2048]{1,0:T(8,128)(2,1)S(1)}, u32[]{:S(2)}, u32[]{:S(2)}) collective-permute-start(bf16[16,2048]{1,0:T(8,128)(2,1)S(1)} %slice.217), channel_id=1, source_target_pairs={{1,0},{2,1},{3,2},{4,3},{5,4},{6,5},{7,6},{8,7},{9,8},{10,9},{11,1... | collective-permute-start | bytes 196616 | tf_op jit(solution)/shard_map/ppermute | solution.py:10
  383.0 5.5 collective-permute-start.22
  390.6 5.2 collective-permute-start.23
  398.2 5.9 collective-permute-start.24
  406.3 107.4 %collective-permute-start.25 = (bf16[1,2048]{1,0:T(2,128)(2,1)S(1)}, bf16[1,2048]{1,0:T(2,128)(2,1)S(1)}, u32[]{:S(2)}, u32[]{:S(2)}) collective-permute-start(bf16[1,2048]{1,0:T(2,128)(2,1)S(1)} %slice.225), channel_id=1, source_target_pairs={{1,0},{2,1},{3,2},{4,3},{5,4},{6,5},{7,6},{8,7},{9,8},{10,9},{11,1... | collective-permute-start | bytes 12296 | tf_op jit(solution)/shard_map/ppermute | solution.py:10
  409.8 275.1 %all-gather.3.cloned.1.call-start = ((), (), s32[]{:S(2)}) async-start(), calls=%async_computation.3 | async-start | bytes 1310720 | tf_op jit(solution)/shard_map/all_gather | solution.py:115
  (116 other events, 6254.4 us)
Sparse Core Ops, SparseCore 0:
  205.3 223.5 reduce-scatter.1
  430.8 36.2 all-gather.2
Sparse Core Ops, SparseCore 1:
  409.9 273.3 all-reduce.1
